TPU v7x, 32 devices: a whole 2x2x4 slice. The times are simulated.
32 devices in a mesh: seq: 8 (over y, x, core), head: 4 (over z).
Axes of the slice: x: 2, y: 2, z: 4, core: 2. Of those that a mesh axis runs over, the one named last changes fastest.
Arguments:
- queries: bfloat16 [8192, 32, 128], P(('seq', 'head')), may hold values from -6 to 6
- keys: bfloat16 [8192, 32, 2, 128], P(('seq', 'head')), may hold values from -6 to 6
- values: bfloat16 [8192, 32, 2, 128], P(('seq', 'head')), may hold values from -6 to 6
- initial_state: float32 [32, 128, 128], P('head'), may hold values from -192 to 192
Outputs:
- mixed: bfloat16 [8192, 32, 128], P(('seq', 'head'))
All inputs are finite; a program needn't handle non-finite values.
Results may differ from a plain program's by a relative error of at most 0.004.
Values may be sent and summed in bfloat16 or wider, within the bound.
A program may use at most 128 MiB of HBM per device.

v0:
```python
import jax
import jax.numpy as jnp
from jax import lax
from jax.sharding import PartitionSpec as P

BLOCK = 64


HIGH = lax.Precision.HIGHEST


def shifted(value, axis, by):
    size = lax.axis_size(axis)
    pairs = [(i, i + by) for i in range(size) if 0 <= i + by < size]
    return lax.ppermute(value, axis, pairs)


def matmul(left, right):
    return jnp.dot(left, right, precision=HIGH, preferred_element_type=jnp.float32)


def batched(left, right):
    return jnp.einsum("hij,hjk->hik", left, right, precision=HIGH)


def unit_rows(raw_keys):
    floats = raw_keys.astype(jnp.float32)
    return floats * lax.rsqrt(jnp.sum(floats * floats, axis=-1, keepdims=True) + 1e-06)


def all_factors(k_blocks, v_blocks):
    updates = k_blocks.shape[2]
    head_width = k_blocks.shape[3]
    gram = jnp.einsum("hbid,hbjd->hbij", k_blocks, k_blocks, precision=HIGH)
    system = jnp.eye(updates, dtype=jnp.float32) + jnp.tril(2.0 * gram, -1)
    solved = lax.linalg.triangular_solve(
        system,
        2.0 * jnp.concatenate([k_blocks, v_blocks], axis=-1),
        left_side=True,
        lower=True,
        unit_diagonal=True,
    )
    return (solved[..., :head_width], solved[..., head_width:])


def visible_scores(q_blk, k_blk):
    rows = q_blk.shape[0]
    updates = k_blk.shape[0]
    per_token = updates // rows
    row_ids = lax.broadcasted_iota(jnp.int32, (rows, updates), 0)
    col_ids = lax.broadcasted_iota(jnp.int32, (rows, updates), 1)
    return jnp.where(col_ids < (row_ids + 1) * per_token, matmul(q_blk, k_blk.T), 0.0)


def start_pair(head_width):
    return jnp.concatenate(
        [jnp.zeros((head_width, head_width), jnp.float32), jnp.eye(head_width, dtype=jnp.float32)],
        axis=1,
    )


def carried_pass(q_blocks, k_blocks, w_blocks, u_blocks):
    head_width = q_blocks.shape[2]

    def advance(pair_state, block_item):
        q_blk, k_blk, w_mat, u_mat = block_item
        feed_rows = jnp.concatenate([u_mat, jnp.zeros_like(u_mat)], axis=1) - matmul(
            w_mat, pair_state
        )
        outputs = matmul(q_blk, pair_state) + matmul(visible_scores(q_blk, k_blk), feed_rows)
        return (pair_state + matmul(k_blk.T, feed_rows), outputs)

    final_pair, outputs = lax.scan(
        advance, start_pair(head_width), (q_blocks, k_blocks, w_blocks, u_blocks)
    )
    outputs = outputs.reshape(-1, 2 * head_width)
    return (
        final_pair[:, head_width:],
        final_pair[:, :head_width],
        outputs[:, :head_width],
        outputs[:, head_width:],
    )


def per_device(queries, keys, values, initial_state):
    q_heads, k_heads, v_heads = (
        lax.all_to_all(queries, "head", split_axis=1, concat_axis=0, tiled=True),
        lax.all_to_all(keys, "head", split_axis=1, concat_axis=0, tiled=True),
        lax.all_to_all(values, "head", split_axis=1, concat_axis=0, tiled=True),
    )
    head_width = q_heads.shape[2]
    local_heads = q_heads.shape[1]
    blocks = q_heads.shape[0] // BLOCK
    q_blocks = jnp.moveaxis(q_heads.astype(jnp.float32), 1, 0).reshape(
        local_heads, blocks, BLOCK, head_width
    )
    k_blocks = jnp.moveaxis(unit_rows(k_heads), 1, 0).reshape(local_heads, blocks, -1, head_width)
    v_blocks = jnp.moveaxis(v_heads.astype(jnp.float32), 1, 0).reshape(
        local_heads, blocks, -1, head_width
    )
    w_blocks, u_blocks = all_factors(k_blocks, v_blocks)
    transition, additive, local_out, query_gain = jax.vmap(carried_pass)(
        q_blocks, k_blocks, w_blocks, u_blocks
    )
    at_first = lax.axis_index("seq") == 0
    start_state = jnp.where(at_first, initial_state, jnp.zeros_like(initial_state))

    def relay_step(loop_step, current):
        passed = shifted(batched(transition, current) + additive, "seq", 1)
        return jnp.where(at_first, initial_state, passed)

    incoming = lax.fori_loop(0, lax.axis_size("seq") - 1, relay_step, start_state)
    raw_out = local_out + batched(query_gain, incoming)
    scaled = raw_out * lax.rsqrt(jnp.mean(raw_out * raw_out, axis=-1, keepdims=True) + 1e-06)
    tokens_major = jnp.moveaxis(scaled.astype(jnp.bfloat16), 0, 1)
    return lax.all_to_all(tokens_major, "head", split_axis=0, concat_axis=1, tiled=True)


def solution(mesh):
    placed = (
        P(("seq", "head"), None, None),
        P(("seq", "head"), None, None, None),
        P(("seq", "head"), None, None, None),
        P("head", None, None),
    )
    return jax.shard_map(
        per_device,
        mesh=mesh,
        in_specs=placed,
        out_specs=P(("seq", "head"), None, None),
        check_vma=False,
    )
```

profile of v0, /device:TPU:7, one launch (start us, length us, event | category | flops | bytes accessed | tf_op | source)
XLA Modules:
  0.0 1862.9 jit_solution(2008826472031273315)
XLA Ops:
  8.3 8.5 copy.65
  16.8 39.3 %all-to-all-done.2 = bf16[256,32,128]{2,0,1:T(8,128)(2,1)S(1)} async-done(((bf16[256,32,128]{2,0,1:T(8,128)(2,1)}), bf16[256,32,128]{2,0,1:T(8,128)(2,1)S(1)}, u32[]{:S(2)}, u32[]{:S(2)}) %all-to-all-start.2) | async-done | bytes 2097184 | tf_op jit(solution)/shard_map/all_to_all | solution.py:87
  62.3 8.5 copy.70
  70.9 84.2 %all-to-all-done = bf16[256,32,2,128]{3,2,0,1:T(2,128)(2,1)} async-done(((bf16[256,32,2,128]{3,2,0,1:T(2,128)(2,1)}), bf16[256,32,2,128]{3,2,0,1:T(2,128)(2,1)}, u32[]{:S(2)}, u32[]{:S(2)}) %all-to-all-start) | async-done | bytes 4194336 | tf_op jit(solution)/shard_map/all_to_all | solution.py:88
  165.5 8.9 convert_element_type.65
  174.4 7.3 copy.66
  181.8 12.6 multiply_reduce_fusion
  199.9 12.5 broadcast_multiply_fusion
  215.6 20.1 %add_bitcast_fusion = f32[8,16,1,128,128]{4,3,2,1,0:T(8,128)} fusion(f32[128,128]{1,0:T(8,128)S(1)} %fusion.23, f32[128,128]{1,0:T(8,128)S(1)} %get-tuple-element.146, pred[128,128]{1,0:T(8,128)(4,1)S(1)} %get-tuple-element.145, f32[8,16,128,128]{3,2,1,0:T(8,128)S(1)} %bitcast.116), kind=kOutput, calls=%fused_computation.32 | convolution fusion | flops 3231711232 | bytes 16924672 | tf_op jit(solution)/shard_map/hbid,hbjd->hbij/dot_general | solution.py:34
  235.7 1259.0 %custom-call.3 = f32[8,16,1,128,128]{3,4,2,1,0:T(8,128)} custom-call(f32[8,16,1,128,128]{4,3,2,1,0:T(8,128)} %add_bitcast_fusion), custom_call_target="InvertDiagBlocksLowerTriangular" | custom-call | tf_op jit(solution)/shard_map/triangular_solve | solution.py:36
  1494.7 8.9 convert_bitcast_fusion
  1503.6 7.3 copy.71
  1510.9 23.9 %fusion.12 = f32[8,16,128,256]{3,2,1,0:T(8,128)} fusion(f32[8,16,128,128]{3,2,1,0:T(8,128)} %bitcast.121, f32[8,16,128,128]{3,2,1,0:T(8,128)} %bitcast.117, f32[8,16,1,128,128]{3,4,2,1,0:T(8,128)} %custom-call.3), kind=kOutput, calls=%fused_computation.24 | convolution fusion | flops 6450839552 | bytes 41943040 | tf_op jit(solution)/shard_map/triangular_solve | solution.py:36
  1534.8 10.8 slice_bitcast_fusion
  1545.7 175.3 %while.22 = (s32[]{:T(128)}, f32[8,128,256]{2,1,0:T(8,128)S(1)}, f32[16,8,64,256]{3,2,1,0:T(8,128)}, f32[16,8,128,128]{3,2,0,1:T(8,128)}, f32[16,8,128,128]{3,2,...) while((s32[]{:T(128)}, f32[8,128,256]{2,1,0:T(8,128)S(1)}, ...), condition=%wide.region_2.3_spmd, body=%wide.region_1.2_spmd.sunk | while | flops 1309352064 | bytes 13650525 | solution.py:73
  1721.1 7.7 copy.81
  1728.8 72.8 %while.23 = (s32[]{:T(128)}, f32[8,128,128]{2,1,0:T(8,128)S(1)}, pred[]{:T(512)}, f32[8,128,128]{2,1,0:T(8,128)S(1)}, f32[8,128,128]{2,1,0:T(8,128)S(1)}, /*index=5*/f32[8,128,128]{2,1,0:T(8,128)S(1)}, s32[]{:T(128)}) while((s32[]{:T(128)}, f32[8,128,128]{2,1,0:T(8,128)S(1)}, pred[]{:T(512)}, f32[8,128,128]{2,1,0:T(8,128)S(1)}, ...), condition=%wide.region_4.5_spmd, body=%wide.region_3.4_spmd.sunk | while | flops 201588736 | bytes 5767286 | solution.py:112
  1736.2 9.2 collective-permute-done
  1747.4 9.2 collective-permute-done
  1758.7 9.2 collective-permute-done
  1769.9 9.2 collective-permute-done
  1781.1 9.2 collective-permute-done
  1792.3 9.2 collective-permute-done
  1811.4 49.7 %all_to_all.45 = bf16[1024,8,128]{2,1,0:T(8,128)(2,1)S(1)} all-to-all(bf16[1024,8,128]{2,1,0:T(8,128)(2,1)S(1)} %copy.84), channel_id=1, replica_groups=mesh['seq'=8,'head'=4] {'head'}, dimensions={0} | all-to-all | bytes 4194304 | tf_op jit(solution)/shard_map/all_to_all | solution.py:116
  (195 shorter events, 236.7 us)
Async XLA Ops:
  3.7 52.3 %all-to-all-start.2 = ((bf16[256,32,128]{2,0,1:T(8,128)(2,1)}), bf16[256,32,128]{2,0,1:T(8,128)(2,1)S(1)}, u32[]{:S(2)}, u32[]{:S(2)}) async-start(bf16[256,32,128]{2,0,1:T(8,128)(2,1)} %copy.73), calls=%async_computation.2 | async-start | bytes 4194304 | tf_op jit(solution)/shard_map/all_to_all | solution.py:87
  56.1 1.3 copy-start.2
  57.4 97.7 %all-to-all-start = ((bf16[256,32,2,128]{3,2,0,1:T(2,128)(2,1)}), bf16[256,32,2,128]{3,2,0,1:T(2,128)(2,1)}, u32[]{:S(2)}, u32[]{:S(2)}) async-start(bf16[256,32,2,128]{3,2,0,1:T(2,128)(2,1)} %copy.65), calls=%async_computation | async-start | bytes 8388608 | tf_op jit(solution)/shard_map/all_to_all | solution.py:88
  62.3 98.0 %copy-start.1 = (f32[8,128,128]{2,1,0:T(8,128)S(1)}, f32[8,128,128]{2,1,0:T(8,128)}, u32[]{:S(2)}) copy-start(f32[8,128,128]{2,1,0:T(8,128)} %param.11) | copy-start | bytes 1572868
  155.1 1339.6 %all-to-all-start.1 = ((bf16[256,32,2,128]{3,2,0,1:T(2,128)(2,1)}), bf16[256,32,2,128]{3,2,0,1:T(2,128)(2,1)}, u32[]{:S(2)}, u32[]{:S(2)}) async-start(bf16[256,32,2,128]{3,2,0,1:T(2,128)(2,1)} %copy.70), calls=%async_computation.1 | async-start | bytes 8388608 | tf_op jit(solution)/shard_map/all_to_all | solution.py:89
  212.4 3.2 copy-start
  1729.5 4.7 collective-permute-start
  1734.9 10.5 collective-permute-start
  1746.1 10.5 collective-permute-start
  1757.4 10.5 collective-permute-start
  1768.6 10.5 collective-permute-start
  1779.8 10.5 collective-permute-start
  1791.0 10.5 collective-permute-start
where the time goes:
time: 1880 us; the launch traced here: 1860 us
  other arithmetic  1310 us (70%)
  matrix products  195 us (10%)
  waiting for transfers between devices  182 us (10%)
  local copies, waits for them, and re-layouts  102 us (5%)
  blocking collectives  49.7 us (3%)
  starting transfers between devices  23.6 us (1%)
    another operation x4, other arithmetic, all_factors(): lax.linalg.triangular_solve(system, 2.0 * jnp.concatenate([k_blocks, v_bl...  1260 us
    dot_general x80, matrix products, matmul(): jnp.dot(left, right, precision=HIGH, preferred_element_type=jnp.float32)  140 us
    all_to_all x1, waiting for transfers between devices, per_device(): lax.all_to_all(keys, 'head', split_axis=1, concat_axis=0, tiled=True)  84.2 us
    ppermute x7, waiting for transfers between devices, shifted(): return lax.ppermute(value, axis, pairs)  58.6 us
    all_to_all x1, blocking collectives, per_device(): lax.all_to_all(tokens_major, 'head', split_axis=0, concat_axis=1, tiled=T...  49.7 us
    all_to_all x1, waiting for transfers between devices, per_device(): lax.all_to_all(queries, 'head', split_axis=1, concat_axis=0, tiled=True)  39.3 us
  transfers between devices with their start and end apart: 10, of which 9 were waited for; matrix products, arithmetic and copies ran while one was open for 72% of the time, Pallas kernels for 0%

commit v1 on v0

--- a/solution.py
+++ b/solution.py
@@ -1,9 +1,302 @@
+import functools
+
 import jax
 import jax.numpy as jnp
 from jax import lax
+from jax.experimental import pallas as pl
+from jax.experimental.pallas import tpu as pltpu
 from jax.sharding import PartitionSpec as P
 
 BLOCK = 64
+BASE = 16
+HEADS_A_STEP = 1
+INBOX_BYTES = 24 << 20
+
+F32 = jnp.float32
+BF16 = jnp.bfloat16
+MESH = pl.DeviceIdType.MESH
+
+
+def mm(left, right, dims=((1,), (0,))):
+    return lax.dot_general(left, right, (dims, ((), ())), preferred_element_type=F32)
+
+
+def split(x):
+    high = x.astype(BF16)
+    return high, (x - high.astype(F32)).astype(BF16)
+
+
+def cat(parts, axis):
+    return jnp.concatenate(parts, axis=axis)
+
+
+def exact_left(left, right):
+    high, low = split(right)
+    return mm(cat([left, left], 1), cat([high, low], 0))
+
+
+def exact_right(left, right):
+    high, low = split(left)
+    return mm(cat([high, low], 1), cat([right, right], 0))
+
+
+def both_split(lh, ll, rh, rl):
+    return mm(cat([lh, ll], 1), cat([rh, rh], 0)) + mm(lh, rl)
+
+
+def both(left, right):
+    return both_split(*split(left), *split(right))
+
+
+def odd_rows(x, size):
+    rows = x.shape[0]
+    return cat([x[s : s + size] for s in range(size, rows, 2 * size)], 0)
+
+
+def merge_rows(even_from, odd, size):
+    rows = even_from.shape[0]
+    parts = []
+    for i, s in enumerate(range(0, rows, 2 * size)):
+        parts += [even_from[s : s + size], odd[i * size : (i + 1) * size]]
+    return cat(parts, 0)
+
+
+def unit_lower_inverse(x):
+    n = x.shape[0]
+    row = lax.broadcasted_iota(jnp.int32, (n, n), 0)
+    col = lax.broadcasted_iota(jnp.int32, (n, n), 1)
+    same = row // BASE == col // BASE
+    inner = jnp.where(same, x, 0.0)
+    packed = inner[:BASE]
+    for s in range(BASE, n, BASE):
+        packed = packed + inner[s : s + BASE]
+    sub = lax.broadcasted_iota(jnp.int32, (BASE, n), 0)
+    lane = lax.broadcasted_iota(jnp.int32, (BASE, n), 1)
+    inv = jnp.where(sub == lane % BASE, 1.0, 0.0)
+    for j in range(BASE - 1):
+        coef = jnp.take_along_axis(packed, lane - lane % BASE + j, axis=1)
+        inv = inv - coef * inv[j : j + 1]
+    m = jnp.where(same, cat([inv] * (n // BASE), 0), 0.0)
+    size = BASE
+    while size < n:
+        below = odd_rows(jnp.where(col // size == row // size - 1, x, 0.0), size)
+        mh, ml = split(m)
+        y = both_split(*split(below), mh, ml)
+        y = merge_rows(jnp.zeros((n, n), F32), y, size)
+        z = both_split(odd_rows(mh, size), odd_rows(ml, size), *split(y))
+        m = merge_rows(m, odd_rows(m, size) - z, size)
+        size *= 2
+    return m
+
+
+def block_factors(q, k, v):
+    n, width = k.shape
+    tokens = q.shape[0]
+    kq = cat([k, q], 0)
+    gs = mm(kq, k, ((1,), (1,)))
+    gram, scores = gs[:n], gs[n:]
+    row = lax.broadcasted_iota(jnp.int32, (n, n), 0)
+    col = lax.broadcasted_iota(jnp.int32, (n, n), 1)
+    diag = jnp.where(row == col, gram, 0.0)
+    d_col = lax.rsqrt(jnp.sum(diag, axis=1, keepdims=True) + 1e-06)
+    d_row = lax.rsqrt(jnp.sum(diag, axis=0, keepdims=True) + 1e-06)
+    x = jnp.where(col < row, (2.0 * d_col) * gram * d_row, 0.0)
+    scaled = unit_lower_inverse(x) * (2.0 * d_col)
+    trow = lax.broadcasted_iota(jnp.int32, (tokens, n), 0)
+    tcol = lax.broadcasted_iota(jnp.int32, (tokens, n), 1)
+    seen = jnp.where(tcol < (trow + 1) * (n // tokens), scores, 0.0)
+    return kq, scaled * d_row, exact_right(scaled, v), seen
+
+
+def local_kernel(q_ref, k_ref, v_ref, pair_ref, local_ref, gain_ref):
+    heads, tokens, width = q_ref.shape
+    per_token = k_ref.shape[1] // tokens
+    step = min(BLOCK, tokens)
+    n = step * per_token
+    for h in range(heads):
+        factors = []
+        for b in range(tokens // step):
+            k = k_ref[h, b * n : (b + 1) * n]
+            q = q_ref[h, b * step : (b + 1) * step]
+            v = v_ref[h, b * n : (b + 1) * n]
+            factors.append((k,) + block_factors(q, k, v))
+        row = lax.broadcasted_iota(jnp.int32, (width, width), 0)
+        col = lax.broadcasted_iota(jnp.int32, (width, width), 1)
+        eye = jnp.where(row == col, 1.0, 0.0)
+        pair = cat([jnp.zeros((width, width), F32), eye], 1)
+        for b, (k, kq, near, fed, seen) in enumerate(factors):
+            if b == 0:
+                q = kq[n:].astype(F32)
+                passed = cat([jnp.zeros_like(q), q], 1)
+                feed = cat([fed, -exact_right(near, k)], 1)
+            else:
+                ahead = exact_left(kq, pair)
+                passed = ahead[n:]
+                feed = cat([fed, jnp.zeros_like(fed)], 1) - both(near, ahead[:n])
+            fh, fl = split(feed)
+            out = passed + both_split(*split(seen), fh, fl)
+            pair = pair + mm(cat([k, k], 0), cat([fh, fl], 0), ((0,), (0,)))
+            local_ref[h, b * step : (b + 1) * step] = out[:, :width]
+            gain_ref[h, b * step : (b + 1) * step] = out[:, width:]
+        pair_ref[h] = pair
+
+
+def local_pass(q, k, v):
+    heads, tokens, width = q.shape
+    g = HEADS_A_STEP
+
+    def spec(rows, columns):
+        return pl.BlockSpec((g, rows, columns), lambda i: (i, 0, 0))
+
+    return pl.pallas_call(
+        local_kernel,
+        grid=(heads // g,),
+        in_specs=[spec(tokens, width), spec(k.shape[1], width), spec(k.shape[1], width)],
+        out_specs=[spec(width, 2 * width), spec(tokens, width), spec(tokens, width)],
+        out_shape=[
+            jax.ShapeDtypeStruct((heads, width, 2 * width), F32),
+            jax.ShapeDtypeStruct((heads, tokens, width), F32),
+            jax.ShapeDtypeStruct((heads, tokens, width), F32),
+        ],
+        name="local_pass",
+    )(q, k, v)
+
+
+def relay_kernel(
+    ns, nh, pair_ref, init_ref, sin_ref, inbox, states, send, recv, send_state, recv_state
+):
+    si, zi = lax.axis_index("seq"), lax.axis_index("head")
+    me = si * nh + zi
+    n = ns * nh
+    mine = zi * ns + si
+    width = init_ref.shape[1]
+
+    def place(p):
+        return p // nh, lax.rem(p, nh)
+
+    barrier = pltpu.get_barrier_semaphore()
+
+    @pl.loop(1, n)
+    def _(i):
+        pl.semaphore_signal(
+            barrier, inc=1, device_id=place(lax.rem(me + i, n)), device_id_type=MESH
+        )
+
+    pl.semaphore_wait(barrier, n - 1)
+
+    def pair_copy(i):
+        ps, pz = place(lax.rem(me + i, n))
+        return pltpu.make_async_remote_copy(
+            src_ref=pair_ref.at[pz * ns + ps],
+            dst_ref=inbox.at[me],
+            send_sem=send.at[i],
+            recv_sem=recv.at[me],
+            device_id=(ps, pz),
+            device_id_type=MESH,
+        )
+
+    def state_copy(d):
+        return pltpu.make_async_remote_copy(
+            src_ref=states.at[d],
+            dst_ref=sin_ref.at[mine],
+            send_sem=send_state.at[d],
+            recv_sem=recv_state.at[mine],
+            device_id=place(d),
+            device_id_type=MESH,
+        )
+
+    @pl.loop(1, n)
+    def _(i):
+        pair_copy(i).start()
+
+    pltpu.make_async_copy(pair_ref.at[mine], inbox.at[me], recv.at[me]).start()
+
+    def advance(d, state):
+        states[d] = state.astype(states.dtype)
+
+        @pl.when(d != me)
+        def _():
+            state_copy(d).start()
+
+        @pl.when(d == me)
+        def _():
+            pltpu.make_async_copy(states.at[d], sin_ref.at[mine], recv_state.at[mine]).start()
+
+        pltpu.make_async_copy(inbox.at[d], inbox.at[d], recv.at[d]).wait()
+        pair = inbox[d]
+        return both(pair[:, width:], state) + pair[:, :width]
+
+    lax.fori_loop(0, n, advance, init_ref[si])
+
+    @pl.loop(1, n)
+    def _(i):
+        pair_copy(i).wait_send()
+
+    @pl.loop(0, n)
+    def _(d):
+        @pl.when(d != me)
+        def _():
+            state_copy(d).wait_send()
+
+    @pl.loop(0, n)
+    def _(h):
+        pltpu.make_async_copy(sin_ref.at[h], sin_ref.at[h], recv_state.at[h]).wait()
+
+
+def relay(pairs, initial_state):
+    ns, nh = lax.axis_size("seq"), lax.axis_size("head")
+    n = ns * nh
+    heads, width, _ = pairs.shape
+    return pl.pallas_call(
+        functools.partial(relay_kernel, ns, nh),
+        in_specs=[pl.BlockSpec(memory_space=pl.ANY), pl.BlockSpec(memory_space=pltpu.VMEM)],
+        out_specs=pl.BlockSpec(memory_space=pl.ANY),
+        out_shape=jax.ShapeDtypeStruct((heads, width, width), F32),
+        scratch_shapes=[
+            pltpu.VMEM((n, width, 2 * width), F32),
+            pltpu.VMEM((n, width, width), F32),
+            pltpu.SemaphoreType.DMA((n,)),
+            pltpu.SemaphoreType.DMA((n,)),
+            pltpu.SemaphoreType.DMA((n,)),
+            pltpu.SemaphoreType.DMA((heads,)),
+        ],
+        compiler_params=pltpu.CompilerParams(collective_id=0, has_side_effects=True),
+        name="relay",
+    )(pairs, initial_state)
+
+
+def finish_kernel(local_ref, gain_ref, state_ref, out_ref):
+    for h in range(local_ref.shape[0]):
+        raw = local_ref[h] + both(gain_ref[h], state_ref[h])
+        mean = jnp.mean(raw * raw, axis=-1, keepdims=True)
+        out_ref[h] = (raw * lax.rsqrt(mean + 1e-06)).astype(out_ref.dtype)
+
+
+def finish(local, gain, state):
+    heads, tokens, width = local.shape
+    g = 4 if heads % 4 == 0 else 1
+
+    def spec(rows):
+        return pl.BlockSpec((g, rows, width), lambda i: (i, 0, 0))
+
+    return pl.pallas_call(
+        finish_kernel,
+        grid=(heads // g,),
+        in_specs=[spec(tokens), spec(tokens), spec(width)],
+        out_specs=spec(tokens),
+        out_shape=jax.ShapeDtypeStruct((heads, tokens, width), BF16),
+        name="finish",
+    )(local, gain, state)
+
+
+def owned_per_device(queries, keys, values, initial_state):
+    tokens, heads, width = queries.shape
+    q = jnp.swapaxes(queries, 0, 1)
+    k = jnp.moveaxis(keys, 1, 0).reshape(heads, -1, width)
+    v = jnp.moveaxis(values, 1, 0).reshape(heads, -1, width)
+    pairs, local, gain = local_pass(q, k, v)
+    incoming = relay(pairs, initial_state)
+    return jnp.swapaxes(finish(local, gain, incoming), 0, 1)
 
 
 HIGH = lax.Precision.HIGHEST
@@ -123,8 +416,17 @@
         P(("seq", "head"), None, None, None),
         P("head", None, None),
     )
+    devices = mesh.shape["seq"] * mesh.shape["head"]
+
+    def chosen(queries, keys, values, initial_state):
+        own_heads, width = initial_state.shape[:2]
+        inbox = devices * 2 * width * width * 4
+        if own_heads == mesh.shape["seq"] and inbox <= INBOX_BYTES:
+            return owned_per_device(queries, keys, values, initial_state)
+        return per_device(queries, keys, values, initial_state)
+
     return jax.shard_map(
-        per_device,
+        chosen,
         mesh=mesh,
         in_specs=placed,
         out_specs=P(("seq", "head"), None, None),

time: 1880 us -> 388 us (0.21)
  other arithmetic: 1310 us -> 0 us
  Pallas kernels: 0 us -> 363 us
  matrix products: 195 us -> 0 us
  waiting for transfers between devices: 182 us -> 0 us
  local copies, waits for them, and re-layouts: 102 us -> 23 us
  blocking collectives: 49.7 us -> 0 us
  starting transfers between devices: 23.6 us -> 0 us
    another operation x4 -> x0, other arithmetic: 1260 us -> none  [all_factors(): lax.linalg.triangular_solve(system, 2.0 * jnp.concatenate([k_blocks, v_bl...]
    pallas_call x0 -> x3, Pallas kernels: none -> 363 us  [the longest x1 210 us: local_pass(): pl.pallas_call(local_kernel, grid=(heads // g,), in_specs=[spec(tokens, w...]
    dot_general x89 -> x0, matrix products: 171 us -> none  [the longest x80 140 us: matmul(): jnp.dot(left, right, precision=HIGH, preferred_element_type=jnp.float32)]
    all_to_all x3 -> x0, waiting for transfers between devices: 124 us -> none  [the longest x1 84.2 us: per_device(): lax.all_to_all(keys, 'head', split_axis=1, concat_axis=0, tiled=True)]
    ppermute x7 -> x0, waiting for transfers between devices: 58.6 us -> none  [shifted(): return lax.ppermute(value, axis, pairs)]
    all_to_all x1 -> x0, blocking collectives: 49.7 us -> none  [per_device(): lax.all_to_all(tokens_major, 'head', split_axis=0, concat_axis=1, tiled=T...]
    another operation x1 -> x0, matrix products: 23.9 us -> none  [all_factors(): lax.linalg.triangular_solve(system, 2.0 * jnp.concatenate([k_blocks, v_bl...]
    unnamed x9 -> x3, local copies, waits for them, and re-layouts: 25.3 us -> 3.87 us
  transfers between devices with their start and end apart: 10 -> 0, of which waited for: 9 -> 0; matrix products, arithmetic and copies ran while one was open for 72% -> 0% of each run, Pallas kernels for 0% -> 0%
where the time goes in v1:
time: 388 us; the launch traced here: 386 us
  Pallas kernels  363 us (94%)
  local copies, waits for them, and re-layouts  23 us (6%)
    pallas_call x1, Pallas kernels, local_pass(): pl.pallas_call(local_kernel, grid=(heads // g,), in_specs=[spec(tokens, w...  210 us
    pallas_call x1, Pallas kernels, relay(): pl.pallas_call(functools.partial(relay_kernel, ns, nh), in_specs=[pl.Bloc...  144 us
    pallas_call x1, Pallas kernels, finish(): pl.pallas_call(finish_kernel, grid=(heads // g,), in_specs=[spec(tokens),...  8.84 us
    transpose x1, local copies, waits for them, and re-layouts, owned_per_device(): v = jnp.moveaxis(values, 1, 0).reshape(heads, -1, width)  8.48 us

profile of v1, /device:TPU:7, one launch (start us, length us, event | category | flops | bytes accessed | tf_op | source)
XLA Modules:
  0.0 386.0 jit_solution(17015156714383677524)
XLA Ops:
  0.0 0.0 copy-start
  0.0 3.9 %copy.10 = bf16[256,32,128]{2,0,1:T(8,128)(2,1)} copy(bf16[256,32,128]{2,1,0:T(8,128)(2,1)} %param.4) | data formatting | bytes 4194304 | tf_op args[0]
  3.9 0.0 copy-done
  3.9 6.4 %copy.6 = bf16[32,256,2,128]{3,2,1,0:T(2,128)(2,1)} copy(bf16[32,256,2,128]{3,2,0,1:T(2,128)(2,1)S(1)} %bitcast.12) | data formatting | bytes 8388608 | tf_op jit(solution)/shard_map/transpose | solution.py:295
  10.3 8.5 %copy.7 = bf16[32,256,2,128]{3,2,1,0:T(2,128)(2,1)} copy(bf16[32,256,2,128]{3,2,0,1:T(2,128)(2,1)} %bitcast.13) | data formatting | bytes 8388608 | tf_op jit(solution)/shard_map/transpose | solution.py:296
  18.8 210.0 %local_pass.1 = (f32[32,128,256]{2,1,0:T(8,128)}, f32[32,256,128]{2,1,0:T(8,128)}, f32[32,256,128]{2,1,0:T(8,128)}) custom-call(bf16[32,256,128]{2,1,0:T(8,128)(2,1)} %bitcast.10, bf16[32,512,128]{2,1,0:T(8,128)(2,1)} %bitcast.8, bf16[32,512,128]{2,1,0:T(8,128)(2,1)} %bitcast.9), custom_call_target="tpu_custom_call" | custom-call | tf_op jit(solution)/shard_map/local_pass/pallas_call | solution.py:151
  228.8 144.1 %relay.1.state_ref = f32[32,128,128]{2,1,0:T(8,128)} custom-call(f32[32,128,256]{2,1,0:T(8,128)} %get-tuple-element.10.pair_ref, f32[8,128,128]{2,1,0:T(8,128)} %init_ref.1), custom_call_target="tpu_custom_call" | custom-call | tf_op jit(solution)/shard_map/relay/pallas_call | solution.py:250
  372.9 8.8 %finish.1 = bf16[32,256,128]{2,1,0:T(8,128)(2,1)} custom-call(f32[32,256,128]{2,1,0:T(8,128)} %get-tuple-element.8.local_ref, f32[32,256,128]{2,1,0:T(8,128)} %get-tuple-element.9.gain_ref, f32[32,128,128]{2,1,0:T(8,128)} %relay.1.state_ref), custom_call_target="tpu_custom_call" | custom-call | tf_op jit(solution)/shard_map/finish/pallas_call | solution.py:282
  381.8 4.3 %copy.8 = bf16[256,32,128]{2,1,0:T(8,128)(2,1)} copy(bf16[256,32,128]{2,0,1:T(8,128)(2,1)} %bitcast.11) | data formatting | bytes 4194304 | tf_op jit(solution)/shard_map/transpose | solution.py:299
Async XLA Ops:
  0.0 3.9 %copy-start = (bf16[256,32,2,128]{3,2,1,0:T(2,128)(2,1)S(1)}, bf16[256,32,2,128]{3,2,1,0:T(2,128)(2,1)}, u32[]{:S(2)}) copy-start(bf16[256,32,2,128]{3,2,1,0:T(2,128)(2,1)} %param.5) | copy-start | bytes 12582916

commit v2 on v1

--- a/solution.py
+++ b/solution.py
@@ -9,7 +9,7 @@
 
 BLOCK = 64
 BASE = 16
-HEADS_A_STEP = 1
+HEADS_A_STEP = 4
 INBOX_BYTES = 24 << 20
 
 F32 = jnp.float32
@@ -61,51 +61,66 @@
     return cat(parts, 0)
 
 
-def unit_lower_inverse(x):
-    n = x.shape[0]
+def unit_lower_inverses(xs):
+    n = xs[0].shape[0]
     row = lax.broadcasted_iota(jnp.int32, (n, n), 0)
     col = lax.broadcasted_iota(jnp.int32, (n, n), 1)
     same = row // BASE == col // BASE
-    inner = jnp.where(same, x, 0.0)
-    packed = inner[:BASE]
-    for s in range(BASE, n, BASE):
-        packed = packed + inner[s : s + BASE]
     sub = lax.broadcasted_iota(jnp.int32, (BASE, n), 0)
     lane = lax.broadcasted_iota(jnp.int32, (BASE, n), 1)
-    inv = jnp.where(sub == lane % BASE, 1.0, 0.0)
+    packs = []
+    for x in xs:
+        inner = jnp.where(same, x, 0.0)
+        packed = inner[:BASE]
+        for s in range(BASE, n, BASE):
+            packed = packed + inner[s : s + BASE]
+        packs.append(packed)
+    invs = [jnp.where(sub == lane % BASE, 1.0, 0.0) for _ in xs]
     for j in range(BASE - 1):
-        coef = jnp.take_along_axis(packed, lane - lane % BASE + j, axis=1)
-        inv = inv - coef * inv[j : j + 1]
-    m = jnp.where(same, cat([inv] * (n // BASE), 0), 0.0)
+        at = lane - lane % BASE + j
+        coefs = [jnp.take_along_axis(packed, at, axis=1) for packed in packs]
+        invs = [inv - coef * inv[j : j + 1] for inv, coef in zip(invs, coefs)]
+    ms = [jnp.where(same, cat([inv] * (n // BASE), 0), 0.0) for inv in invs]
     size = BASE
     while size < n:
-        below = odd_rows(jnp.where(col // size == row // size - 1, x, 0.0), size)
-        mh, ml = split(m)
-        y = both_split(*split(below), mh, ml)
-        y = merge_rows(jnp.zeros((n, n), F32), y, size)
-        z = both_split(odd_rows(mh, size), odd_rows(ml, size), *split(y))
-        m = merge_rows(m, odd_rows(m, size) - z, size)
+        near = col // size == row // size - 1
+        belows = [split(odd_rows(jnp.where(near, x, 0.0), size)) for x in xs]
+        halves = [split(m) for m in ms]
+        ys = [both_split(*below, *half) for below, half in zip(belows, halves)]
+        ys = [split(merge_rows(jnp.zeros((n, n), F32), y, size)) for y in ys]
+        zs = [
+            both_split(odd_rows(mh, size), odd_rows(ml, size), *y)
+            for (mh, ml), y in zip(halves, ys)
+        ]
+        ms = [merge_rows(m, odd_rows(m, size) - z, size) for m, z in zip(ms, zs)]
         size *= 2
-    return m
-
-
-def block_factors(q, k, v):
-    n, width = k.shape
-    tokens = q.shape[0]
-    kq = cat([k, q], 0)
-    gs = mm(kq, k, ((1,), (1,)))
-    gram, scores = gs[:n], gs[n:]
+    return ms
+
+
+def block_factors(blocks):
+    n, width = blocks[0][1].shape
+    tokens = blocks[0][0].shape[0]
     row = lax.broadcasted_iota(jnp.int32, (n, n), 0)
     col = lax.broadcasted_iota(jnp.int32, (n, n), 1)
-    diag = jnp.where(row == col, gram, 0.0)
-    d_col = lax.rsqrt(jnp.sum(diag, axis=1, keepdims=True) + 1e-06)
-    d_row = lax.rsqrt(jnp.sum(diag, axis=0, keepdims=True) + 1e-06)
-    x = jnp.where(col < row, (2.0 * d_col) * gram * d_row, 0.0)
-    scaled = unit_lower_inverse(x) * (2.0 * d_col)
     trow = lax.broadcasted_iota(jnp.int32, (tokens, n), 0)
     tcol = lax.broadcasted_iota(jnp.int32, (tokens, n), 1)
-    seen = jnp.where(tcol < (trow + 1) * (n // tokens), scores, 0.0)
-    return kq, scaled * d_row, exact_right(scaled, v), seen
+    visible = tcol < (trow + 1) * (n // tokens)
+    kqs = [cat([k, q], 0) for q, k, _ in blocks]
+    products = [mm(kq, k, ((1,), (1,))) for kq, (_, k, _) in zip(kqs, blocks)]
+    xs, d_cols, d_rows, seens = [], [], [], []
+    for gs in products:
+        gram = gs[:n]
+        diag = jnp.where(row == col, gram, 0.0)
+        d_col = lax.rsqrt(jnp.sum(diag, axis=1, keepdims=True) + 1e-06)
+        d_row = lax.rsqrt(jnp.sum(diag, axis=0, keepdims=True) + 1e-06)
+        xs.append(jnp.where(col < row, (2.0 * d_col) * gram * d_row, 0.0))
+        d_cols.append(d_col)
+        d_rows.append(d_row)
+        seens.append(split(jnp.where(visible, gs[n:], 0.0)))
+    scaled = [m * (2.0 * d_col) for m, d_col in zip(unit_lower_inverses(xs), d_cols)]
+    feds = [exact_right(m, v) for m, (_, _, v) in zip(scaled, blocks)]
+    nears = [split(m * d_row) for m, d_row in zip(scaled, d_rows)]
+    return kqs, nears, feds, seens
 
 
 def local_kernel(q_ref, k_ref, v_ref, pair_ref, local_ref, gain_ref):
@@ -113,31 +128,50 @@
     per_token = k_ref.shape[1] // tokens
     step = min(BLOCK, tokens)
     n = step * per_token
-    for h in range(heads):
-        factors = []
-        for b in range(tokens // step):
-            k = k_ref[h, b * n : (b + 1) * n]
-            q = q_ref[h, b * step : (b + 1) * step]
-            v = v_ref[h, b * n : (b + 1) * n]
-            factors.append((k,) + block_factors(q, k, v))
-        row = lax.broadcasted_iota(jnp.int32, (width, width), 0)
-        col = lax.broadcasted_iota(jnp.int32, (width, width), 1)
-        eye = jnp.where(row == col, 1.0, 0.0)
-        pair = cat([jnp.zeros((width, width), F32), eye], 1)
-        for b, (k, kq, near, fed, seen) in enumerate(factors):
-            if b == 0:
-                q = kq[n:].astype(F32)
-                passed = cat([jnp.zeros_like(q), q], 1)
-                feed = cat([fed, -exact_right(near, k)], 1)
-            else:
-                ahead = exact_left(kq, pair)
-                passed = ahead[n:]
-                feed = cat([fed, jnp.zeros_like(fed)], 1) - both(near, ahead[:n])
-            fh, fl = split(feed)
-            out = passed + both_split(*split(seen), fh, fl)
-            pair = pair + mm(cat([k, k], 0), cat([fh, fl], 0), ((0,), (0,)))
+    count = tokens // step
+    blocks = [
+        (
+            q_ref[h, b * step : (b + 1) * step],
+            k_ref[h, b * n : (b + 1) * n],
+            v_ref[h, b * n : (b + 1) * n],
+        )
+        for b in range(count)
+        for h in range(heads)
+    ]
+    kqs, nears, feds, seens = block_factors(blocks)
+    row = lax.broadcasted_iota(jnp.int32, (width, width), 0)
+    col = lax.broadcasted_iota(jnp.int32, (width, width), 1)
+    eye = jnp.where(row == col, 1.0, 0.0)
+    pairs = [cat([jnp.zeros((width, width), F32), eye], 1)] * heads
+    for b in range(count):
+        at = slice(b * heads, (b + 1) * heads)
+        if b == 0:
+            qs = [kq[n:].astype(F32) for kq in kqs[at]]
+            passed = [cat([jnp.zeros_like(q), q], 1) for q in qs]
+            feeds = [
+                cat([fed, -mm(cat(list(near), 1), cat([kq[:n], kq[:n]], 0))], 1)
+                for fed, near, kq in zip(feds[at], nears[at], kqs[at])
+            ]
+        else:
+            aheads = [exact_left(kq, pair) for kq, pair in zip(kqs[at], pairs)]
+            passed = [ahead[n:] for ahead in aheads]
+            feeds = [
+                cat([fed, jnp.zeros_like(fed)], 1) - both_split(*near, *split(ahead[:n]))
+                for fed, near, ahead in zip(feds[at], nears[at], aheads)
+            ]
+        feeds = [split(feed) for feed in feeds]
+        pairs = [
+            pair + mm(cat([kq[:n], kq[:n]], 0), cat(list(feed), 0), ((0,), (0,)))
+            for pair, kq, feed in zip(pairs, kqs[at], feeds)
+        ]
+        outs = [
+            base + both_split(*seen, *feed)
+            for base, seen, feed in zip(passed, seens[at], feeds)
+        ]
+        for h, out in enumerate(outs):
             local_ref[h, b * step : (b + 1) * step] = out[:, :width]
             gain_ref[h, b * step : (b + 1) * step] = out[:, width:]
+    for h, pair in enumerate(pairs):
         pair_ref[h] = pair
 
 

time: 388 us -> 232 us (0.60)
  Pallas kernels: 363 us -> 207 us
    pallas_call x1, Pallas kernels: 210 us -> 54 us  [local_pass(): pl.pallas_call(local_kernel, grid=(heads // g,), in_specs=[spec(tokens, w...]
where the time goes in v2:
time: 232 us; the launch traced here: 230 us
  Pallas kernels  207 us (89%)
  local copies, waits for them, and re-layouts  23 us (10%)
    pallas_call x1, Pallas kernels, relay(): pl.pallas_call(functools.partial(relay_kernel, ns, nh), in_specs=[pl.Bloc...  144 us
    pallas_call x1, Pallas kernels, local_pass(): pl.pallas_call(local_kernel, grid=(heads // g,), in_specs=[spec(tokens, w...  54 us
    pallas_call x1, Pallas kernels, finish(): pl.pallas_call(finish_kernel, grid=(heads // g,), in_specs=[spec(tokens),...  8.84 us
    transpose x1, local copies, waits for them, and re-layouts, owned_per_device(): v = jnp.moveaxis(values, 1, 0).reshape(heads, -1, width)  8.48 us
    transpose x1, local copies, waits for them, and re-layouts, owned_per_device(): k = jnp.moveaxis(keys, 1, 0).reshape(heads, -1, width)  6.4 us

profile of v2, /device:TPU:7, one launch (start us, length us, event | category | flops | bytes accessed | tf_op | source)
XLA Modules:
  0.0 229.9 jit_solution(10527342036936117738)
XLA Ops:
  0.0 0.0 copy-start
  0.0 3.9 %copy.10 = bf16[256,32,128]{2,0,1:T(8,128)(2,1)} copy(bf16[256,32,128]{2,1,0:T(8,128)(2,1)} %param.4) | data formatting | bytes 4194304 | tf_op args[0]
  3.9 0.0 copy-done
  3.9 6.4 %copy.6 = bf16[32,256,2,128]{3,2,1,0:T(2,128)(2,1)} copy(bf16[32,256,2,128]{3,2,0,1:T(2,128)(2,1)S(1)} %bitcast.12) | data formatting | bytes 8388608 | tf_op jit(solution)/shard_map/transpose | solution.py:329
  10.3 8.5 %copy.7 = bf16[32,256,2,128]{3,2,1,0:T(2,128)(2,1)} copy(bf16[32,256,2,128]{3,2,0,1:T(2,128)(2,1)} %bitcast.13) | data formatting | bytes 8388608 | tf_op jit(solution)/shard_map/transpose | solution.py:330
  18.8 54.0 %local_pass.1 = (f32[32,128,256]{2,1,0:T(8,128)}, f32[32,256,128]{2,1,0:T(8,128)}, f32[32,256,128]{2,1,0:T(8,128)}) custom-call(bf16[32,256,128]{2,1,0:T(8,128)(2,1)} %bitcast.10, bf16[32,512,128]{2,1,0:T(8,128)(2,1)} %bitcast.8, bf16[32,512,128]{2,1,0:T(8,128)(2,1)} %bitcast.9), custom_call_target="tpu_custom_call" | custom-call | tf_op jit(solution)/shard_map/local_pass/pallas_call | solution.py:185
  72.7 144.1 %relay.1.state_ref = f32[32,128,128]{2,1,0:T(8,128)} custom-call(f32[32,128,256]{2,1,0:T(8,128)} %get-tuple-element.10.pair_ref, f32[8,128,128]{2,1,0:T(8,128)} %init_ref.1), custom_call_target="tpu_custom_call" | custom-call | tf_op jit(solution)/shard_map/relay/pallas_call | solution.py:284
  216.8 8.8 %finish.1 = bf16[32,256,128]{2,1,0:T(8,128)(2,1)} custom-call(f32[32,256,128]{2,1,0:T(8,128)} %get-tuple-element.8.local_ref, f32[32,256,128]{2,1,0:T(8,128)} %get-tuple-element.9.gain_ref, f32[32,128,128]{2,1,0:T(8,128)} %relay.1.state_ref), custom_call_target="tpu_custom_call" | custom-call | tf_op jit(solution)/shard_map/finish/pallas_call | solution.py:316
  225.7 4.3 %copy.8 = bf16[256,32,128]{2,1,0:T(8,128)(2,1)} copy(bf16[256,32,128]{2,0,1:T(8,128)(2,1)} %bitcast.11) | data formatting | bytes 4194304 | tf_op jit(solution)/shard_map/transpose | solution.py:333
Async XLA Ops:
  0.0 3.9 %copy-start = (bf16[256,32,2,128]{3,2,1,0:T(2,128)(2,1)S(1)}, bf16[256,32,2,128]{3,2,1,0:T(2,128)(2,1)}, u32[]{:S(2)}) copy-start(bf16[256,32,2,128]{3,2,1,0:T(2,128)(2,1)} %param.5) | copy-start | bytes 12582916

commit v3 on v2

--- a/solution.py
+++ b/solution.py
@@ -11,6 +11,7 @@
 BASE = 16
 HEADS_A_STEP = 4
 INBOX_BYTES = 24 << 20
+VMEM_BYTES = 56 << 20
 
 F32 = jnp.float32
 BF16 = jnp.bfloat16
@@ -123,7 +124,7 @@
     return kqs, nears, feds, seens
 
 
-def local_kernel(q_ref, k_ref, v_ref, pair_ref, local_ref, gain_ref):
+def local_maps(q_ref, k_ref, v_ref, local_ref, gain_ref, first):
     heads, tokens, width = q_ref.shape
     per_token = k_ref.shape[1] // tokens
     step = min(BLOCK, tokens)
@@ -169,158 +170,190 @@
             for base, seen, feed in zip(passed, seens[at], feeds)
         ]
         for h, out in enumerate(outs):
-            local_ref[h, b * step : (b + 1) * step] = out[:, :width]
-            gain_ref[h, b * step : (b + 1) * step] = out[:, width:]
-    for h, pair in enumerate(pairs):
-        pair_ref[h] = pair
-
-
-def local_pass(q, k, v):
-    heads, tokens, width = q.shape
-    g = HEADS_A_STEP
-
-    def spec(rows, columns):
-        return pl.BlockSpec((g, rows, columns), lambda i: (i, 0, 0))
-
-    return pl.pallas_call(
-        local_kernel,
-        grid=(heads // g,),
-        in_specs=[spec(tokens, width), spec(k.shape[1], width), spec(k.shape[1], width)],
-        out_specs=[spec(width, 2 * width), spec(tokens, width), spec(tokens, width)],
-        out_shape=[
-            jax.ShapeDtypeStruct((heads, width, 2 * width), F32),
-            jax.ShapeDtypeStruct((heads, tokens, width), F32),
-            jax.ShapeDtypeStruct((heads, tokens, width), F32),
-        ],
-        name="local_pass",
-    )(q, k, v)
-
-
-def relay_kernel(
-    ns, nh, pair_ref, init_ref, sin_ref, inbox, states, send, recv, send_state, recv_state
+            local_ref[first + h, b * step : (b + 1) * step] = out[:, :width]
+            gain_ref[first + h, b * step : (b + 1) * step] = out[:, width:]
+    return pairs
+
+
+def group_of(step, ns, nh, size):
+    own = (lax.axis_index("head") * ns + lax.axis_index("seq")) // size
+    groups = ns * nh // size
+    return lax.rem(own + 1 + step, groups)
+
+
+def mixer_kernel(
+    ns,
+    nh,
+    q_ref,
+    k_ref,
+    v_ref,
+    init_ref,
+    out_ref,
+    local,
+    gain,
+    t_out,
+    a_out,
+    t_box,
+    a_box,
+    states,
+    incoming,
+    t_send,
+    a_send,
+    t_recv,
+    a_recv,
+    s_send,
+    s_recv,
 ):
+    size, tokens, width = q_ref.shape
+    step = pl.program_id(0)
     si, zi = lax.axis_index("seq"), lax.axis_index("head")
     me = si * nh + zi
     n = ns * nh
     mine = zi * ns + si
-    width = init_ref.shape[1]
 
     def place(p):
         return p // nh, lax.rem(p, nh)
 
-    barrier = pltpu.get_barrier_semaphore()
-
-    @pl.loop(1, n)
-    def _(i):
-        pl.semaphore_signal(
-            barrier, inc=1, device_id=place(lax.rem(me + i, n)), device_id_type=MESH
-        )
-
-    pl.semaphore_wait(barrier, n - 1)
-
-    def pair_copy(i):
-        ps, pz = place(lax.rem(me + i, n))
-        return pltpu.make_async_remote_copy(
-            src_ref=pair_ref.at[pz * ns + ps],
-            dst_ref=inbox.at[me],
-            send_sem=send.at[i],
-            recv_sem=recv.at[me],
-            device_id=(ps, pz),
-            device_id_type=MESH,
-        )
+    def owner(head):
+        return lax.rem(head, ns), head // ns
+
+    def map_copies(head):
+        return [
+            pltpu.make_async_remote_copy(
+                src_ref=src.at[head],
+                dst_ref=box.at[me],
+                send_sem=send.at[head],
+                recv_sem=recv.at[me],
+                device_id=owner(head),
+                device_id_type=MESH,
+            )
+            for src, box, send, recv in (
+                (t_out, t_box, t_send, t_recv),
+                (a_out, a_box, a_send, a_recv),
+            )
+        ]
 
     def state_copy(d):
         return pltpu.make_async_remote_copy(
             src_ref=states.at[d],
-            dst_ref=sin_ref.at[mine],
-            send_sem=send_state.at[d],
-            recv_sem=recv_state.at[mine],
+            dst_ref=incoming.at[mine],
+            send_sem=s_send.at[d],
+            recv_sem=s_recv.at[mine],
             device_id=place(d),
             device_id_type=MESH,
         )
 
-    @pl.loop(1, n)
-    def _(i):
-        pair_copy(i).start()
-
-    pltpu.make_async_copy(pair_ref.at[mine], inbox.at[me], recv.at[me]).start()
-
-    def advance(d, state):
-        states[d] = state.astype(states.dtype)
-
-        @pl.when(d != me)
+    @pl.when(step == 0)
+    def _():
+        barrier = pltpu.get_barrier_semaphore()
+
+        @pl.loop(1, n)
+        def _(i):
+            pl.semaphore_signal(
+                barrier, inc=1, device_id=place(lax.rem(me + i, n)), device_id_type=MESH
+            )
+
+        pl.semaphore_wait(barrier, n - 1)
+
+    first = group_of(step, ns, nh, size) * size
+    pairs = local_maps(q_ref, k_ref, v_ref, local, gain, first)
+    for h, pair in enumerate(pairs):
+        t_out[first + h] = pair[:, width:]
+        a_out[first + h] = pair[:, :width].astype(a_out.dtype)
+
+    @pl.loop(first, first + size)
+    def _(head):
+        @pl.when(head != mine)
         def _():
-            state_copy(d).start()
-
-        @pl.when(d == me)
+            for copy in map_copies(head):
+                copy.start()
+
+        @pl.when(head == mine)
         def _():
-            pltpu.make_async_copy(states.at[d], sin_ref.at[mine], recv_state.at[mine]).start()
-
-        pltpu.make_async_copy(inbox.at[d], inbox.at[d], recv.at[d]).wait()
-        pair = inbox[d]
-        return both(pair[:, width:], state) + pair[:, :width]
-
-    lax.fori_loop(0, n, advance, init_ref[si])
-
-    @pl.loop(1, n)
-    def _(i):
-        pair_copy(i).wait_send()
-
-    @pl.loop(0, n)
-    def _(d):
-        @pl.when(d != me)
-        def _():
-            state_copy(d).wait_send()
-
-    @pl.loop(0, n)
-    def _(h):
-        pltpu.make_async_copy(sin_ref.at[h], sin_ref.at[h], recv_state.at[h]).wait()
-
-
-def relay(pairs, initial_state):
+            pltpu.make_async_copy(t_out.at[mine], t_box.at[me], t_recv.at[me]).start()
+            pltpu.make_async_copy(a_out.at[mine], a_box.at[me], a_recv.at[me]).start()
+
+    @pl.when(step == pl.num_programs(0) - 1)
+    def _():
+        def advance(d, state):
+            states[d] = state.astype(states.dtype)
+
+            @pl.when(d != me)
+            def _():
+                state_copy(d).start()
+
+            @pl.when(d == me)
+            def _():
+                pltpu.make_async_copy(
+                    states.at[d], incoming.at[mine], s_recv.at[mine]
+                ).start()
+
+            pltpu.make_async_copy(t_box.at[d], t_box.at[d], t_recv.at[d]).wait()
+            pltpu.make_async_copy(a_box.at[d], a_box.at[d], a_recv.at[d]).wait()
+            return both(t_box[d], state) + a_box[d].astype(F32)
+
+        lax.fori_loop(0, n, advance, init_ref[si])
+
+        @pl.loop(0, n // size)
+        def _(g):
+            heads = [g * size + h for h in range(size)]
+            for head in heads:
+                pltpu.make_async_copy(
+                    incoming.at[head], incoming.at[head], s_recv.at[head]
+                ).wait()
+            for head in heads:
+                raw = local[head] + exact_right(gain[head], incoming[head])
+                mean = jnp.mean(raw * raw, axis=-1, keepdims=True)
+                out_ref[head] = (raw * lax.rsqrt(mean + 1e-06)).astype(out_ref.dtype)
+
+        @pl.loop(0, n)
+        def _(head):
+            @pl.when(head != mine)
+            def _():
+                for copy in map_copies(head):
+                    copy.wait_send()
+
+            @pl.when(head != me)
+            def _():
+                state_copy(head).wait_send()
+
+
+def mixer(q, k, v, initial_state):
     ns, nh = lax.axis_size("seq"), lax.axis_size("head")
-    n = ns * nh
-    heads, width, _ = pairs.shape
+    heads, tokens, width = q.shape
+    g = HEADS_A_STEP
+
+    def spec(rows):
+        return pl.BlockSpec((g, rows, width), lambda i: (group_of(i, ns, nh, g), 0, 0))
+
+    square = (heads, width, width)
     return pl.pallas_call(
-        functools.partial(relay_kernel, ns, nh),
-        in_specs=[pl.BlockSpec(memory_space=pl.ANY), pl.BlockSpec(memory_space=pltpu.VMEM)],
-        out_specs=pl.BlockSpec(memory_space=pl.ANY),
-        out_shape=jax.ShapeDtypeStruct((heads, width, width), F32),
+        functools.partial(mixer_kernel, ns, nh),
+        grid=(heads // g,),
+        in_specs=[
+            spec(tokens),
+            spec(k.shape[1]),
+            spec(k.shape[1]),
+            pl.BlockSpec(initial_state.shape, lambda i: (0, 0, 0)),
+        ],
+        out_specs=pl.BlockSpec((heads, tokens, width), lambda i: (0, 0, 0)),
+        out_shape=jax.ShapeDtypeStruct((heads, tokens, width), BF16),
         scratch_shapes=[
-            pltpu.VMEM((n, width, 2 * width), F32),
-            pltpu.VMEM((n, width, width), F32),
-            pltpu.SemaphoreType.DMA((n,)),
-            pltpu.SemaphoreType.DMA((n,)),
-            pltpu.SemaphoreType.DMA((n,)),
-            pltpu.SemaphoreType.DMA((heads,)),
-        ],
-        compiler_params=pltpu.CompilerParams(collective_id=0, has_side_effects=True),
-        name="relay",
-    )(pairs, initial_state)
-
-
-def finish_kernel(local_ref, gain_ref, state_ref, out_ref):
-    for h in range(local_ref.shape[0]):
-        raw = local_ref[h] + both(gain_ref[h], state_ref[h])
-        mean = jnp.mean(raw * raw, axis=-1, keepdims=True)
-        out_ref[h] = (raw * lax.rsqrt(mean + 1e-06)).astype(out_ref.dtype)
-
-
-def finish(local, gain, state):
-    heads, tokens, width = local.shape
-    g = 4 if heads % 4 == 0 else 1
-
-    def spec(rows):
-        return pl.BlockSpec((g, rows, width), lambda i: (i, 0, 0))
-
-    return pl.pallas_call(
-        finish_kernel,
-        grid=(heads // g,),
-        in_specs=[spec(tokens), spec(tokens), spec(width)],
-        out_specs=spec(tokens),
-        out_shape=jax.ShapeDtypeStruct((heads, tokens, width), BF16),
-        name="finish",
-    )(local, gain, state)
+            pltpu.VMEM((heads, tokens, width), F32),
+            pltpu.VMEM((heads, tokens, width), F32),
+            pltpu.VMEM(square, F32),
+            pltpu.VMEM(square, BF16),
+            pltpu.VMEM(square, F32),
+            pltpu.VMEM(square, BF16),
+            pltpu.VMEM(square, BF16),
+            pltpu.VMEM(square, BF16),
+        ]
+        + [pltpu.SemaphoreType.DMA((heads,))] * 6,
+        compiler_params=pltpu.CompilerParams(
+            collective_id=0, has_side_effects=True, vmem_limit_bytes=VMEM_BYTES
+        ),
+        name="mixer",
+    )(q, k, v, initial_state)
 
 
 def owned_per_device(queries, keys, values, initial_state):
@@ -328,9 +361,7 @@
     q = jnp.swapaxes(queries, 0, 1)
     k = jnp.moveaxis(keys, 1, 0).reshape(heads, -1, width)
     v = jnp.moveaxis(values, 1, 0).reshape(heads, -1, width)
-    pairs, local, gain = local_pass(q, k, v)
-    incoming = relay(pairs, initial_state)
-    return jnp.swapaxes(finish(local, gain, incoming), 0, 1)
+    return jnp.swapaxes(mixer(q, k, v, initial_state), 0, 1)
 
 
 HIGH = lax.Precision.HIGHEST

time: 232 us -> 151 us (0.65)
  Pallas kernels: 207 us -> 127 us
    pallas_call x3 -> x1, Pallas kernels: 207 us -> 127 us  [mixer(): pl.pallas_call(functools.partial(mixer_kernel, ns, nh), grid=(heads // g,...]
where the time goes in v3:
time: 151 us; the launch traced here: 150 us
  Pallas kernels  127 us (84%)
  local copies, waits for them, and re-layouts  23 us (15%)
    pallas_call x1, Pallas kernels, mixer(): pl.pallas_call(functools.partial(mixer_kernel, ns, nh), grid=(heads // g,...  127 us
    transpose x1, local copies, waits for them, and re-layouts, owned_per_device(): v = jnp.moveaxis(values, 1, 0).reshape(heads, -1, width)  8.51 us
    transpose x1, local copies, waits for them, and re-layouts, owned_per_device(): k = jnp.moveaxis(keys, 1, 0).reshape(heads, -1, width)  6.39 us
    transpose x1, local copies, waits for them, and re-layouts, owned_per_device(): return jnp.swapaxes(mixer(q, k, v, initial_state), 0, 1)  4.26 us
    unnamed x3, local copies, waits for them, and re-layouts  3.87 us

profile of v3, /device:TPU:7, one launch (start us, length us, event | category | flops | bytes accessed | tf_op | source)
XLA Modules:
  0.0 150.4 jit_solution(15606694817356327388)
XLA Ops:
  0.0 0.0 copy-start
  0.0 3.9 %copy.10 = bf16[256,32,128]{2,0,1:T(8,128)(2,1)} copy(bf16[256,32,128]{2,1,0:T(8,128)(2,1)} %param.4) | data formatting | bytes 4194304 | tf_op args[0]
  3.9 0.0 copy-done
  3.9 6.4 %copy.6 = bf16[32,256,2,128]{3,2,1,0:T(2,128)(2,1)} copy(bf16[32,256,2,128]{3,2,0,1:T(2,128)(2,1)S(1)} %bitcast.12) | data formatting | bytes 8388608 | tf_op jit(solution)/shard_map/transpose | solution.py:362
  10.3 8.5 %copy.7 = bf16[32,256,2,128]{3,2,1,0:T(2,128)(2,1)} copy(bf16[32,256,2,128]{3,2,0,1:T(2,128)(2,1)} %bitcast.13) | data formatting | bytes 8388608 | tf_op jit(solution)/shard_map/transpose | solution.py:363
  18.8 127.3 %mixer.1 = bf16[32,256,128]{2,1,0:T(8,128)(2,1)} custom-call(bf16[32,256,128]{2,1,0:T(8,128)(2,1)} %bitcast.11, bf16[32,512,128]{2,1,0:T(8,128)(2,1)} %bitcast.8, bf16[32,512,128]{2,1,0:T(8,128)(2,1)} %bitcast.9, f32[8,128,128]{2,1,0:T(8,128)} %init_ref.1), custom_call_target="tpu_custom_call" | custom-call | tf_op jit(solution)/shard_map/mixer/pallas_call | solution.py:330
  146.1 4.3 %copy.8 = bf16[256,32,128]{2,1,0:T(8,128)(2,1)} copy(bf16[256,32,128]{2,0,1:T(8,128)(2,1)} %bitcast.10) | data formatting | bytes 4194304 | tf_op jit(solution)/shard_map/transpose | solution.py:364
Async XLA Ops:
  0.0 3.9 %copy-start = (bf16[256,32,2,128]{3,2,1,0:T(2,128)(2,1)S(1)}, bf16[256,32,2,128]{3,2,1,0:T(2,128)(2,1)}, u32[]{:S(2)}) copy-start(bf16[256,32,2,128]{3,2,1,0:T(2,128)(2,1)} %param.5) | copy-start | bytes 12582916

commit v4 on v3

--- a/solution.py
+++ b/solution.py
@@ -9,7 +9,7 @@
 
 BLOCK = 64
 BASE = 16
-HEADS_A_STEP = 4
+HEADS_A_STEP = 8
 INBOX_BYTES = 24 << 20
 VMEM_BYTES = 56 << 20
 
@@ -126,15 +126,15 @@
 
 def local_maps(q_ref, k_ref, v_ref, local_ref, gain_ref, first):
     heads, tokens, width = q_ref.shape
-    per_token = k_ref.shape[1] // tokens
+    per_token = k_ref.shape[2]
     step = min(BLOCK, tokens)
     n = step * per_token
     count = tokens // step
     blocks = [
         (
             q_ref[h, b * step : (b + 1) * step],
-            k_ref[h, b * n : (b + 1) * n],
-            v_ref[h, b * n : (b + 1) * n],
+            k_ref[b * step : (b + 1) * step, h].reshape(n, width),
+            v_ref[b * step : (b + 1) * step, h].reshape(n, width),
         )
         for b in range(count)
         for h in range(heads)
@@ -326,14 +326,19 @@
     def spec(rows):
         return pl.BlockSpec((g, rows, width), lambda i: (group_of(i, ns, nh, g), 0, 0))
 
+    def by_token(rows):
+        return pl.BlockSpec(
+            (tokens, g, rows, width), lambda i: (0, group_of(i, ns, nh, g), 0, 0)
+        )
+
     square = (heads, width, width)
     return pl.pallas_call(
         functools.partial(mixer_kernel, ns, nh),
         grid=(heads // g,),
         in_specs=[
             spec(tokens),
-            spec(k.shape[1]),
-            spec(k.shape[1]),
+            by_token(k.shape[2]),
+            by_token(k.shape[2]),
             pl.BlockSpec(initial_state.shape, lambda i: (0, 0, 0)),
         ],
         out_specs=pl.BlockSpec((heads, tokens, width), lambda i: (0, 0, 0)),
@@ -359,9 +364,7 @@
 def owned_per_device(queries, keys, values, initial_state):
     tokens, heads, width = queries.shape
     q = jnp.swapaxes(queries, 0, 1)
-    k = jnp.moveaxis(keys, 1, 0).reshape(heads, -1, width)
-    v = jnp.moveaxis(values, 1, 0).reshape(heads, -1, width)
-    return jnp.swapaxes(mixer(q, k, v, initial_state), 0, 1)
+    return jnp.swapaxes(mixer(q, keys, values, initial_state), 0, 1)
 
 
 HIGH = lax.Precision.HIGHEST

time: 151 us -> 134 us (0.89)
  local copies, waits for them, and re-layouts: 23 us -> 7.98 us
    transpose x3 -> x1, local copies, waits for them, and re-layouts: 19.2 us -> 4.26 us  [owned_per_device(): return jnp.swapaxes(mixer(q, keys, values, initial_state), 0, 1)]
    pallas_call x1, Pallas kernels: 127 us -> 126 us  [mixer(): pl.pallas_call(functools.partial(mixer_kernel, ns, nh), grid=(heads // g,...]
    unnamed x3 -> x1, local copies, waits for them, and re-layouts: 3.87 us -> 3.72 us
where the time goes in v4:
time: 134 us
  Pallas kernels  126 us (94%)
  local copies, waits for them, and re-layouts  7.98 us (6%)
    pallas_call x1, Pallas kernels, mixer(): pl.pallas_call(functools.partial(mixer_kernel, ns, nh), grid=(heads // g,...  126 us
    transpose x1, local copies, waits for them, and re-layouts, owned_per_device(): return jnp.swapaxes(mixer(q, keys, values, initial_state), 0, 1)  4.26 us
    unnamed x1, local copies, waits for them, and re-layouts  3.72 us

profile of v4, /device:TPU:7, one launch (start us, length us, event | category | flops | bytes accessed | tf_op | source)
XLA Modules:
  0.0 133.7 jit_solution(12932104451351434329)
XLA Ops:
  0.0 3.7 %copy.8 = bf16[256,32,128]{2,0,1:T(8,128)(2,1)} copy(bf16[256,32,128]{2,1,0:T(8,128)(2,1)} %param.4) | data formatting | bytes 4194304 | tf_op args[0]
  3.7 125.7 %mixer.1 = bf16[32,256,128]{2,1,0:T(8,128)(2,1)} custom-call(bf16[32,256,128]{2,1,0:T(8,128)(2,1)} %bitcast.5, bf16[256,32,2,128]{3,2,1,0:T(2,128)(2,1)} %k_ref.1, bf16[256,32,2,128]{3,2,1,0:T(2,128)(2,1)} %v_ref.1, f32[8,128,128]{2,1,0:T(8,128)} %init_ref.1), custom_call_target="tpu_custom_call" | custom-call | tf_op jit(solution)/shard_map/mixer/pallas_call | solution.py:335
  129.4 4.3 %copy.6 = bf16[256,32,128]{2,1,0:T(8,128)(2,1)} copy(bf16[256,32,128]{2,0,1:T(8,128)(2,1)} %bitcast.4) | data formatting | bytes 4194304 | tf_op jit(solution)/shard_map/transpose | solution.py:367
